TPU v7x, 256 devices: a whole 4x4x8 slice. The times are simulated.
256 devices in a mesh: ctx: 32 (over y, z), ch: 8 (over x, core).
Axes of the slice: x: 4, y: 4, z: 8, core: 2. Of those that a mesh axis runs over, the one named last changes fastest.
Arguments:
- queries: float32 [8, 1, 524288], P('ch', None, 'ctx'), may hold values from -6 to 6
- keys: float32 [8, 1, 524288], P('ch', None, 'ctx'), may hold values from -6 to 6
- values: float32 [8, 1, 524288], P('ch', None, 'ctx'), may hold values from -6 to 6
- filters: float32 [1, 524288], P(None, 'ctx'), may hold values from -4 to 4
- cotangent: float32 [8, 1, 524288], P('ch', None, 'ctx'), may hold values from -6 to 6
Outputs:
- mixer_out: float32 [8, 1, 524288], P('ch', None, 'ctx')
- query_grad: float32 [8, 1, 524288], P('ch', None, 'ctx')
- key_grad: float32 [8, 1, 524288], P('ch', None, 'ctx')
- value_grad: float32 [8, 1, 524288], P('ch', None, 'ctx')
- filter_grad: float32 [1, 524288], P(None, ('ctx', 'ch'))
All inputs are finite; a program needn't handle non-finite values.
Results may differ from a plain program's by a relative error of at most 0.00013.
Values sent between devices are 32-bit elements; how exact they have to be, the bound alone decides.
A program may use at most 64 MiB of HBM per device.

v0:
```python
import functools
import math

import jax
import jax.numpy as jnp
import ml_dtypes
import numpy as np
from jax import lax
from jax.experimental import pallas as pl
from jax.experimental.pallas import tpu as pltpu
from jax.sharding import PartitionSpec as P

LANES = 128
OWN = 4
MESH = pl.DeviceIdType.MESH
BF16 = jnp.bfloat16


def split(table):
    high = table.astype(ml_dtypes.bfloat16)
    low = (table - high.astype(np.float64)).astype(ml_dtypes.bfloat16)
    return high, low


def tables(blocks):
    rows = blocks * OWN
    length = rows * LANES
    row = np.arange(2 * rows)
    freq = (row // 8) * OWN + row % OWN + 0.25
    imag = (row % 8) >= OWN
    angle = 2.0 * np.pi * freq[:, None] * np.arange(rows)[None, :] / rows
    outer = np.where(imag[:, None], -np.sin(angle), np.cos(angle))
    high, low = split(outer)
    outer_fwd = np.concatenate([high, low, high], axis=1)
    high, low = split(outer.T / length)
    outer_inv = np.concatenate([high, low, high], axis=1)
    lane = np.arange(LANES)
    twist = 2.0 * np.pi * freq[:, None] * lane[None, :] / length
    twist_cos = np.cos(twist).astype(np.float32)
    twist_sin = np.where(imag[:, None], -np.sin(twist), np.sin(twist)).astype(np.float32)
    inner = 2.0 * np.pi * ((lane[:, None] * lane[None, :]) % LANES) / LANES
    high, low = split(np.concatenate([np.cos(inner), np.sin(inner)], axis=1))
    inner_table = np.concatenate([high, high, low], axis=0)
    return outer_fwd, outer_inv, twist_cos, twist_sin, inner_table


def halves(value):
    high = value.astype(BF16)
    low = (value - high.astype(jnp.float32)).astype(BF16)
    return high, low


def dot(lhs, rhs):
    return jnp.dot(lhs, rhs, preferred_element_type=jnp.float32)


def left_product(table, value):
    high, low = halves(value)
    return dot(table, jnp.concatenate([high, high, low], axis=0))


def right_product(value, table):
    high, low = halves(value)
    return dot(jnp.concatenate([high, low, high], axis=1), table)


def swap(value):
    if value.ndim == 3:
        return pltpu.roll(value, OWN, 1)
    return pltpu.roll(value.reshape(-1, 8, LANES), OWN, 1).reshape(value.shape)


def kernel(
    steps, blocks, members, scale,
    query_ref, key_ref, value_ref, filter_ref, cotangent_ref,
    fwd_ref, inv_ref, cos_ref, sin_ref, inner_ref,
    mixer_ref, query_grad_ref, key_grad_ref, value_grad_ref, filter_grad_ref,
    spectra, arrived, results, returned, grads, filters, mixed, terms, shares,
    send_sems, recv_sems,
):
    me = lax.axis_index("ctx")
    member = lax.axis_index("ch")

    barrier = pltpu.get_barrier_semaphore()
    for step in steps:
        pl.semaphore_signal(
            barrier, inc=1, device_id={"ctx": lax.rem(me + step, blocks)}, device_id_type=MESH
        )
    for step in range(1, members):
        pl.semaphore_signal(
            barrier, inc=1, device_id={"ch": lax.rem(member + step, members)}, device_id_type=MESH
        )

    half = lax.broadcasted_iota(jnp.int32, (1, 8, LANES), 1) < OWN
    sign = jnp.where(half, 1.0, -1.0).astype(jnp.float32)
    row_sign = jnp.broadcast_to(sign, (2 * blocks // 2, 8, LANES)).reshape(-1, LANES)

    def forward(value):
        rows = left_product(fwd_ref[...], value)
        rows = cos_ref[...] * rows + sin_ref[...] * swap(rows)
        both = right_product(rows, inner_ref[...])
        return both[:, :LANES] + row_sign * swap(both[:, LANES:])

    def inverse(rows):
        both = right_product(rows, inner_ref[...])
        rows = both[:, :LANES] - row_sign * swap(both[:, LANES:])
        rows = cos_ref[...] * rows - sin_ref[...] * swap(rows)
        return left_product(inv_ref[...], rows)

    def exchange(source, target, slot, part):
        copies = []
        for at, step in enumerate(steps):
            peer = lax.rem(me + step, blocks)
            copies.append(
                pltpu.make_async_remote_copy(
                    src_ref=source.at[peer, part],
                    dst_ref=target.at[me, part],
                    send_sem=send_sems.at[slot, at],
                    recv_sem=recv_sems.at[slot, at],
                    device_id={"ctx": peer},
                    device_id_type=MESH,
                )
            )
        return copies

    mixed_input = key_ref[...] * value_ref[...]
    grad_in = cotangent_ref[...] * query_ref[...]
    for at, value in enumerate((mixed_input, grad_in, filter_ref[...])):
        spectra[:, at] = forward(value).reshape(blocks, 8, LANES)

    pl.semaphore_wait(barrier, blocks + members - 2)

    sent = exchange(spectra, arrived, 0, pl.ds(0, 3))
    for copy in sent:
        copy.start()
    arrived[me] = spectra[me]

    group = min(8, blocks)
    zeros = jnp.zeros((group, 8, LANES), jnp.float32)
    for copy in sent:
        copy.wait_recv()

    def shifted(value):
        before = jnp.concatenate([jnp.zeros_like(value[:1]), value[:-1]], axis=0)
        return value - sign * swap(before)

    def factors(value):
        other = swap(value)
        return jnp.where(half, value, other), sign * jnp.where(half, other, value)

    grad = arrived[:, 1]
    grads[0, :blocks] = grad
    grads[1, :blocks] = swap(grad)
    grads[0, blocks:] = zeros
    grads[1, blocks:] = zeros
    mix = arrived[:, 0]
    mixed[0, :group] = zeros
    mixed[1, :group] = zeros
    mixed[0, group:] = mix
    mixed[1, group:] = swap(mix)
    real, imag = factors(shifted(mix))
    terms[0] = real
    terms[1] = imag
    real, imag = factors(shifted(arrived[:, 2]))
    filters[0] = real
    filters[1] = imag

    def correlate(factor, first):
        def add(at, total):
            window = pl.ds(first + at, group)
            return total + grads[0, window] * factor[0, at] + grads[1, window] * factor[1, at]
        return lax.fori_loop(0, blocks - first, add, zeros)

    def convolve(first):
        def add(at, total):
            window = pl.ds(group + first - at, group)
            return total + mixed[0, window] * filters[0, at] - mixed[1, window] * filters[1, at]
        return lax.fori_loop(0, first + group, add, zeros)

    for first in range(0, blocks, group):
        results[pl.ds(first, group), 0] = correlate(terms, first)
    sent_terms = exchange(results, returned, 1, pl.ds(0, 1))
    for copy in sent_terms:
        copy.start()
    for first in range(0, blocks, group):
        results[pl.ds(first, group), 1] = convolve(first)
        results[pl.ds(first, group), 2] = correlate(filters, first)
    sent_results = exchange(results, returned, 2, pl.ds(1, 2))
    for copy in sent_results:
        copy.start()
    returned[me] = results[me]

    for copy in sent_terms:
        copy.wait_recv()
    term = inverse(returned[:, 0].reshape(-1, LANES)) * scale
    shares[0] = term.reshape((members,) + shares.shape[2:])
    sent_shares = []
    for step in range(1, members):
        peer = lax.rem(member + step, members)
        sent_shares.append(
            pltpu.make_async_remote_copy(
                src_ref=shares.at[0, peer],
                dst_ref=shares.at[1, step],
                send_sem=send_sems.at[3, step],
                recv_sem=recv_sems.at[3, step],
                device_id={"ch": peer},
                device_id_type=MESH,
            )
        )
    for copy in sent_shares:
        copy.start()

    for copy in sent_results:
        copy.wait_recv()
    convolved = inverse(returned[:, 1].reshape(-1, LANES))
    mixer_ref[...] = query_ref[...] * convolved
    query_grad_ref[...] = cotangent_ref[...] * convolved
    mixed_grad = inverse(returned[:, 2].reshape(-1, LANES))
    key_grad_ref[...] = mixed_grad * value_ref[...]
    value_grad_ref[...] = mixed_grad * key_ref[...]

    total = shares[0, member]
    for copy in sent_shares:
        copy.wait_recv()
    for step in range(1, members):
        total = total + shares[1, step]
    filter_grad_ref[...] = total
    for copy in sent + sent_terms + sent_results + sent_shares:
        copy.wait_send()


def body(queries, keys, values, filters, cotangent):
    blocks = lax.axis_size("ctx")
    members = lax.axis_size("ch")
    rows = blocks * OWN
    share = rows // members
    group = min(8, blocks)
    tokens = queries.shape[-1]
    scale = (members * queries.shape[0] * blocks * tokens) ** -0.5
    steps = list(range(1, blocks))
    block = jax.ShapeDtypeStruct((rows, LANES), jnp.float32)
    view = lambda array: array.reshape(rows, LANES)
    vmem = pl.BlockSpec(memory_space=pltpu.VMEM)
    outputs = pl.pallas_call(
        functools.partial(kernel, steps, blocks, members, scale),
        out_shape=[block] * 4 + [jax.ShapeDtypeStruct((share, LANES), jnp.float32)],
        in_specs=[vmem] * 10,
        out_specs=[vmem] * 5,
        scratch_shapes=[
            pltpu.VMEM((blocks, 3, 8, LANES), jnp.float32),
            pltpu.VMEM((blocks, 3, 8, LANES), jnp.float32),
            pltpu.VMEM((blocks, 3, 8, LANES), jnp.float32),
            pltpu.VMEM((blocks, 3, 8, LANES), jnp.float32),
            pltpu.VMEM((2, blocks + group, 8, LANES), jnp.float32),
            pltpu.VMEM((2, blocks, 8, LANES), jnp.float32),
            pltpu.VMEM((2, blocks + group, 8, LANES), jnp.float32),
            pltpu.VMEM((2, blocks, 8, LANES), jnp.float32),
            pltpu.VMEM((2, members, share, LANES), jnp.float32),
            pltpu.SemaphoreType.DMA((4, blocks)),
            pltpu.SemaphoreType.DMA((4, blocks)),
        ],
        compiler_params=pltpu.CompilerParams(collective_id=0, has_side_effects=True),
    )(*map(view, (queries, keys, values, filters, cotangent)), *map(jnp.asarray, tables(blocks)))
    mixer_out, query_grad, key_grad, value_grad, filter_grad = outputs
    full = lambda array: array.reshape(queries.shape)
    return (
        full(mixer_out), full(query_grad), full(key_grad), full(value_grad),
        filter_grad.reshape(1, tokens // members),
    )


def solution(mesh):
    placed = (
        P("ch", None, "ctx"),
        P("ch", None, "ctx"),
        P("ch", None, "ctx"),
        P(None, "ctx"),
        P("ch", None, "ctx"),
    )
    return jax.shard_map(
        body,
        mesh=mesh,
        in_specs=placed,
        out_specs=(
            P("ch", None, "ctx"),
            P("ch", None, "ctx"),
            P("ch", None, "ctx"),
            P("ch", None, "ctx"),
            P(None, ("ctx", "ch")),
        ),
        check_vma=False,
    )
```

profile of v0, /device:TPU:1, one launch (start us, length us, event | category | flops | bytes accessed | tf_op | source)
XLA Modules:
  0.0 45.7 jit_solution(11856279432741895747)
XLA Ops:
  0.6 40.6 %shard_map.137 = (f32[128,128]{1,0:T(8,128)}, f32[128,128]{1,0:T(8,128)}, f32[128,128]{1,0:T(8,128)}, f32[128,128]{1,0:T(8,128)}, f32[16,128]{1,0:T(8,128)}) custom-call(f32[128,128]{1,0:T(8,128)} %bitcast.10, f32[128,128]{1,0:T(8,128)} %bitcast.11, f32[128,128]{1,0:T(8,128)} %bitcast.12, f32[128,128]{1,0:T(8,128)} %bitcast.13, f32[128,128]{1,0:T(8,128)} %bitcast.14, ...), custom_call_target="tpu_custom_call" | custom-call | tf_op jit(solution)/shard_map/pallas_call | solution.py:244
  41.2 0.0 copy-start.2
  41.2 1.5 %copy.20 = f32[1,1,16384]{2,1,0:T(1,128)} copy(f32[1,1,16384]{2,1,0:T(1,128)} %bitcast.18) | data formatting | bytes 131072
  42.7 0.0 copy-done.2
  42.7 0.0 copy-start.1
  42.7 0.6 %copy.21 = f32[1,1,16384]{2,1,0:T(1,128)} copy(f32[1,1,16384]{2,1,0:T(1,128)S(1)} %bitcast.17) | data formatting | bytes 131072
  43.4 0.2 copy-done.1
  43.6 0.0 copy-start
  43.6 0.6 %copy.22 = f32[1,1,16384]{2,1,0:T(1,128)} copy(f32[1,1,16384]{2,1,0:T(1,128)S(1)} %bitcast.16) | data formatting | bytes 131072
  44.2 0.2 copy-done
  44.5 0.0 copy-start.3
  44.5 0.6 %copy.23 = f32[1,1,16384]{2,1,0:T(1,128)} copy(f32[1,1,16384]{2,1,0:T(1,128)S(1)} %bitcast.15) | data formatting | bytes 131072
  45.1 0.1 copy-done.3
  45.1 0.6 %copy.24 = f32[1,2048]{1,0:T(1,128)} copy(f32[1,2048]{1,0:T(1,128)S(1)} %bitcast.19) | data formatting | bytes 16384
Async XLA Ops:
  41.2 1.5 %copy-start.2 = (f32[128,128]{1,0:T(8,128)S(1)}, f32[128,128]{1,0:T(8,128)}, u32[]{:S(2)}) copy-start(f32[128,128]{1,0:T(8,128)} %get-tuple-element.11) | copy-start | bytes 196612
  42.7 0.9 %copy-start.1 = (f32[128,128]{1,0:T(8,128)S(1)}, f32[128,128]{1,0:T(8,128)}, u32[]{:S(2)}) copy-start(f32[128,128]{1,0:T(8,128)} %get-tuple-element.12) | copy-start | bytes 196612
  43.6 0.9 %copy-start = (f32[128,128]{1,0:T(8,128)S(1)}, f32[128,128]{1,0:T(8,128)}, u32[]{:S(2)}) copy-start(f32[128,128]{1,0:T(8,128)} %get-tuple-element.13) | copy-start | bytes 196612
  44.5 0.7 %copy-start.3 = (f32[16,128]{1,0:T(8,128)S(1)}, f32[16,128]{1,0:T(8,128)}, u32[]{:S(2)}) copy-start(f32[16,128]{1,0:T(8,128)} %get-tuple-element.14) | copy-start | bytes 24580
where the time goes:
time: 46 us; the launch traced here: 45.7 us
  Pallas kernels  40.6 us (88%)
  local copies, waits for them, and re-layouts  4.53 us (10%)
  between operations  0.65 us (1%)
    pallas_call x1, Pallas kernels, body(): pl.pallas_call(functools.partial(kernel, steps, blocks, members, scale),...  40.6 us
    unnamed x13, local copies, waits for them, and re-layouts  4.53 us

commit v1 on v0

v1 whole, which is shorter than its diff:
```python
import functools
import math

import jax
import jax.numpy as jnp
import ml_dtypes
import numpy as np
from jax import lax
from jax.experimental import pallas as pl
from jax.experimental.pallas import tpu as pltpu
from jax.sharding import PartitionSpec as P

LANES = 128
OWN = 4
MESH = pl.DeviceIdType.MESH
BF16 = jnp.bfloat16


def split(table):
    high = table.astype(ml_dtypes.bfloat16)
    low = (table - high.astype(np.float64)).astype(ml_dtypes.bfloat16)
    return high, low


def tables(blocks):
    rows = blocks * OWN
    length = rows * LANES
    row = np.arange(2 * rows)
    freq = (row // 8) * OWN + row % OWN + 0.25
    imag = (row % 8) >= OWN
    angle = 2.0 * np.pi * freq[:, None] * np.arange(rows)[None, :] / rows
    outer = np.where(imag[:, None], -np.sin(angle), np.cos(angle))
    high, low = split(outer)
    outer_fwd = np.concatenate([high, low, high], axis=1)
    high, low = split(outer.T / length)
    outer_inv = np.concatenate([high, low, high], axis=1)
    lane = np.arange(LANES)
    twist = 2.0 * np.pi * freq[:, None] * lane[None, :] / length
    twist_cos = np.cos(twist).astype(np.float32)
    twist_sin = np.where(imag[:, None], -np.sin(twist), np.sin(twist)).astype(np.float32)
    inner = 2.0 * np.pi * ((lane[:, None] * lane[None, :]) % LANES) / LANES
    high, low = split(np.concatenate([np.cos(inner), np.sin(inner)], axis=1))
    inner_table = np.concatenate([high, high, low], axis=0)
    return outer_fwd, outer_inv, twist_cos, twist_sin, inner_table


def halves(value):
    high = value.astype(BF16)
    low = (value - high.astype(jnp.float32)).astype(BF16)
    return high, low


def dot(lhs, rhs):
    return jnp.dot(lhs, rhs, preferred_element_type=jnp.float32)


def left_product(table, value):
    high, low = halves(value)
    return dot(table, jnp.concatenate([high, high, low], axis=0))


def right_product(value, table):
    high, low = halves(value)
    return dot(jnp.concatenate([high, low, high], axis=1), table)


def swap(value):
    if value.ndim == 3:
        return pltpu.roll(value, OWN, 1)
    return pltpu.roll(value.reshape(-1, 8, LANES), OWN, 1).reshape(value.shape)


def kernel(
    blocks, members, scale,
    query_hbm, key_hbm, value_hbm, filter_hbm, cotangent_hbm,
    fwd_hbm, inv_hbm, cos_hbm, sin_hbm, inner_hbm,
    convolved_ref, mixed_grad_ref, filter_grad_ref,
    query_ref, key_ref, value_ref, filter_ref, cotangent_ref,
    fwd_ref, inv_ref, cos_ref, sin_ref, inner_ref,
    spectra, arrived, filter_spectra, filter_arrived,
    results, returned, terms, terms_arrived, term_sums, term_rows, pieces, piece,
    grads, filters, mixed, factor,
    load_sems, pair_send, pair_recv, filter_send, filter_recv, pass_send, pass_recv,
    terms_send, terms_recv, sums_send, sums_recv, result_send, result_recv, piece_send, piece_recv,
):
    me = lax.axis_index("ctx")
    member = lax.axis_index("ch")
    depth = members
    height = blocks // depth
    at_y = lax.div(me, depth)
    at_z = lax.rem(me, depth)

    barrier = pltpu.get_barrier_semaphore()
    for step in range(1, blocks):
        pl.semaphore_signal(
            barrier, inc=1, device_id={"ctx": lax.rem(me + step, blocks)}, device_id_type=MESH
        )
    for step in range(1, members):
        pl.semaphore_signal(
            barrier, inc=1, device_id={"ch": lax.rem(member + step, members)}, device_id_type=MESH
        )

    loads = [
        pltpu.make_async_copy(source, target, load_sems.at[at])
        for at, (source, target) in enumerate((
            (key_hbm, key_ref), (value_hbm, value_ref), (cotangent_hbm, cotangent_ref),
            (query_hbm, query_ref), (fwd_hbm, fwd_ref), (filter_hbm, filter_ref),
            (cos_hbm, cos_ref), (sin_hbm, sin_ref), (inner_hbm, inner_ref), (inv_hbm, inv_ref),
        ))
    ]
    for load in loads:
        load.start()

    half = lax.broadcasted_iota(jnp.int32, (1, 8, LANES), 1) < OWN
    sign = jnp.where(half, 1.0, -1.0).astype(jnp.float32)

    def rows_sign(rows):
        return jnp.broadcast_to(sign, (rows // 8, 8, LANES)).reshape(rows, LANES)

    def forward(values):
        count = len(values)
        rows = left_product(fwd_ref[...], jnp.concatenate(values, axis=1))
        cos, sin = cos_ref[...], sin_ref[...]
        parts = [rows[:, at * LANES : (at + 1) * LANES] for at in range(count)]
        parts = [cos * part + sin * swap(part) for part in parts]
        both = right_product(jnp.concatenate(parts, axis=0), inner_ref[...])
        rows = both[:, :LANES] + rows_sign(count * 8 * blocks) * swap(both[:, LANES:])
        return rows.reshape(count, blocks, 8, LANES)

    def inverse(rows):
        both = right_product(rows, inner_ref[...])
        rows = both[:, :LANES] - rows_sign(8 * blocks) * swap(both[:, LANES:])
        rows = cos_ref[...] * rows - sin_ref[...] * swap(rows)
        return left_product(inv_ref[...], rows)

    def send(source, target, send_sem, recv_sem, **device):
        return pltpu.make_async_remote_copy(
            src_ref=source, dst_ref=target, send_sem=send_sem, recv_sem=recv_sem,
            device_id=device, device_id_type=MESH,
        )

    for load in loads[:9]:
        load.wait()
    mixed_input = key_ref[...] * value_ref[...]
    grad_in = cotangent_ref[...] * query_ref[...]
    filter_spectra[...] = forward([filter_ref[...]])[0]
    pair = forward([mixed_input, grad_in])
    spectra[:, 0] = pair[0]
    spectra[:, 1] = pair[1]

    pl.semaphore_wait(barrier, blocks + members - 2)

    target_z = lax.rem(at_z + member, depth)
    direct = []
    for step in range(height):
        peer = lax.rem(at_y + step, height) * depth + target_z
        direct.append(
            send(
                filter_spectra.at[peer], filter_arrived.at[at_z, at_y],
                filter_send.at[step], filter_recv.at[step], ctx=peer,
            )
        )
    for copy in direct[1:]:
        copy.start()

    @pl.when(member == 0)
    def _():
        filter_arrived[at_z, at_y] = filter_spectra[me]

    @pl.when(member != 0)
    def _():
        direct[0].start()

    pairs = []
    for step in range(1, blocks):
        peer = lax.rem(me + step, blocks)
        pairs.append(
            send(
                spectra.at[peer], arrived.at[me],
                pair_send.at[step], pair_recv.at[step], ctx=peer,
            )
        )
    for copy in pairs:
        copy.start()
    arrived[me] = spectra[me]

    @pl.when(member != 0)
    def _():
        direct[0].wait_recv()

    for copy in direct[1:]:
        copy.wait_recv()
    source_z = lax.rem(at_z - member + depth, depth)
    passed = []
    for step in range(1, members):
        passed.append(
            send(
                filter_arrived.at[source_z], filter_arrived.at[source_z],
                pass_send.at[step], pass_recv.at[step], ch=lax.rem(member + step, members),
            )
        )
    for copy in passed:
        copy.start()

    zeros = jnp.zeros((depth, 8, LANES), jnp.float32)
    grads[0, blocks:] = zeros
    grads[1, blocks:] = zeros
    mixed[0, :depth] = zeros
    mixed[1, :depth] = zeros

    def shifted(value):
        before = jnp.concatenate([jnp.zeros_like(value[:1]), value[:-1]], axis=0)
        return value - sign * swap(before)

    def factors(value):
        other = swap(value)
        return jnp.where(half, value, other), sign * jnp.where(half, other, value)

    unroll = math.gcd(4, depth)

    def correlate(factor, first):
        def add(at, total):
            for more in range(unroll):
                lag = at * unroll + more
                window = pl.ds(first + lag, depth)
                total = total + grads[0, window] * factor[0, lag] + grads[1, window] * factor[1, lag]
            return total
        return lax.fori_loop(0, (blocks - first) // unroll, add, zeros)

    def convolve(first):
        def add(at, total):
            for more in range(unroll):
                lag = at * unroll + more
                window = pl.ds(depth + first - lag, depth)
                total = total + mixed[0, window] * filters[0, lag] - mixed[1, window] * filters[1, lag]
            return total
        return lax.fori_loop(0, (first + depth) // unroll, add, zeros)

    for copy in pairs:
        copy.wait_recv()
    grad = arrived[:, 1]
    grads[0, :blocks] = grad
    grads[1, :blocks] = swap(grad)
    mix = arrived[:, 0]
    mixed[0, depth:] = mix
    mixed[1, depth:] = swap(mix)
    real, imag = factors(shifted(mix))
    factor[0] = real
    factor[1] = imag
    for row in range(height):
        terms[:, row] = correlate(factor, row * depth)
    reduced = []
    for step in range(1, members):
        peer = lax.rem(member + step, members)
        reduced.append(
            send(
                terms.at[peer], terms_arrived.at[step],
                terms_send.at[step], terms_recv.at[step], ch=peer,
            )
        )
    for copy in reduced:
        copy.start()

    for copy in passed:
        copy.wait_recv()
    whole = jnp.concatenate([filter_arrived[:, row] for row in range(height)], axis=0)
    real, imag = factors(shifted(whole))
    filters[0] = real
    filters[1] = imag

    def give_back(part):
        copies = []
        for step in range(1, blocks):
            peer = lax.rem(me + step, blocks)
            copies.append(
                send(
                    results.at[part, peer], returned.at[part, me],
                    result_send.at[part, step], result_recv.at[part, step], ctx=peer,
                )
            )
        for copy in copies:
            copy.start()
        returned[part, me] = results[part, me]
        return copies

    for row in range(height):
        results[0, pl.ds(row * depth, depth)] = convolve(row * depth)
    sent_convolved = give_back(0)

    worker = at_z == member
    for copy in reduced:
        copy.wait_recv()
    total = terms[member]
    for step in range(1, members):
        total = total + terms_arrived[step]
    term_sums[...] = total
    summed = []
    for step in range(height):
        row = lax.rem(at_y + step, height)
        summed.append(
            send(
                term_sums.at[row], term_rows.at[me],
                sums_send.at[step], sums_recv.at[me], ctx=row * depth + member,
            )
        )
    for copy in summed[1:]:
        copy.start()

    @pl.when(worker)
    def _():
        term_rows[me] = term_sums[at_y]

    @pl.when(jnp.logical_not(worker))
    def _():
        summed[0].start()

    for row in range(height):
        results[1, pl.ds(row * depth, depth)] = correlate(filters, row * depth)
    sent_grads = give_back(1)

    loads[9].wait()
    for copy in sent_convolved:
        copy.wait_recv()
    convolved_ref[...] = inverse(returned[0].reshape(-1, LANES))

    scattered = []
    for step in range(1, members):
        peer = lax.rem(member + step, members)
        scattered.append(
            send(pieces.at[peer], piece, piece_send.at[step], piece_recv.at[0], ch=peer)
        )

    @pl.when(worker)
    def _():
        for step in range(1, blocks):
            peer = lax.rem(me + step, blocks)
            send(
                term_sums.at[0], term_rows.at[peer], sums_send.at[0], sums_recv.at[peer], ctx=peer
            ).wait_recv()
        term = inverse(term_rows[...].reshape(-1, LANES)) * scale
        pieces[...] = term.reshape(pieces.shape)
        for copy in scattered:
            copy.start()
        piece[...] = pieces[member]

    for copy in sent_grads:
        copy.wait_recv()
    mixed_grad_ref[...] = inverse(returned[1].reshape(-1, LANES))

    @pl.when(jnp.logical_not(worker))
    def _():
        scattered[0].wait_recv()
        summed[0].wait_send()

    filter_grad_ref[...] = piece[...]

    @pl.when(worker)
    def _():
        for copy in scattered:
            copy.wait_send()

    @pl.when(member != 0)
    def _():
        direct[0].wait_send()

    for copy in direct[1:] + pairs + passed + reduced + sent_convolved + summed[1:] + sent_grads:
        copy.wait_send()


def body(queries, keys, values, filters, cotangent):
    blocks = lax.axis_size("ctx")
    members = lax.axis_size("ch")
    height = blocks // members
    rows = blocks * OWN
    share = rows // members
    tokens = queries.shape[-1]
    scale = (members * queries.shape[0] * blocks * tokens) ** -0.5
    view = lambda array: array.reshape(rows, LANES)
    arrays = [*map(view, (queries, keys, values, filters, cotangent)), *map(jnp.asarray, tables(blocks))]
    anywhere = pl.BlockSpec(memory_space=pl.ANY)
    vmem = lambda *shape: pltpu.VMEM(shape + (8, LANES), jnp.float32)
    dma = lambda *shape: pltpu.SemaphoreType.DMA(shape)
    convolved, mixed_grad, filter_grad = pl.pallas_call(
        functools.partial(kernel, blocks, members, scale),
        out_shape=[pltpu.VMEM((rows, LANES), jnp.float32)] * 2
        + [pltpu.VMEM((share, LANES), jnp.float32)],
        in_specs=[anywhere] * 10,
        out_specs=[pl.BlockSpec(memory_space=pltpu.VMEM)] * 3,
        scratch_shapes=[pltpu.VMEM(array.shape, array.dtype) for array in arrays]
        + [
            vmem(blocks, 2), vmem(blocks, 2), vmem(blocks), vmem(members, height),
            vmem(2, blocks), vmem(2, blocks),
            vmem(members, height), vmem(members, height), vmem(height), vmem(blocks),
            pltpu.VMEM((members, share, LANES), jnp.float32),
            pltpu.VMEM((share, LANES), jnp.float32),
            vmem(2, blocks + members), vmem(2, blocks), vmem(2, blocks + members), vmem(2, blocks),
            dma(10), dma(blocks), dma(blocks), dma(height), dma(height), dma(members), dma(members),
            dma(members), dma(members), dma(height), dma(blocks), dma(2, blocks), dma(2, blocks),
            dma(members), dma(1),
        ],
        compiler_params=pltpu.CompilerParams(collective_id=0, has_side_effects=True),
    )(*arrays)
    convolved = convolved.reshape(queries.shape)
    mixed_grad = mixed_grad.reshape(queries.shape)
    return (
        queries * convolved, cotangent * convolved, mixed_grad * values, mixed_grad * keys,
        filter_grad.reshape(1, tokens // members),
    )


def solution(mesh):
    placed = (
        P("ch", None, "ctx"),
        P("ch", None, "ctx"),
        P("ch", None, "ctx"),
        P(None, "ctx"),
        P("ch", None, "ctx"),
    )
    return jax.shard_map(
        body,
        mesh=mesh,
        in_specs=placed,
        out_specs=(
            P("ch", None, "ctx"),
            P("ch", None, "ctx"),
            P("ch", None, "ctx"),
            P("ch", None, "ctx"),
            P(None, ("ctx", "ch")),
        ),
        check_vma=False,
    )
```

time: 46 us -> 39.7 us (0.86)
  local copies, waits for them, and re-layouts: 4.53 us -> 0.62 us
  Pallas kernels: 40.6 us -> 36.9 us
  other arithmetic: 0 us -> 0.92 us
    unnamed x13 -> x9, local copies, waits for them, and re-layouts: 4.53 us -> 0.62 us
    pallas_call x1, Pallas kernels: 40.6 us -> 36.9 us  [body(): pl.pallas_call(functools.partial(kernel, blocks, members, scale), out_sha...]
    mul x0 -> x1, other arithmetic: none -> 0.92 us  [body(): mixed_grad * keys]
where the time goes in v1:
time: 39.7 us; the launch traced here: 39.2 us
  Pallas kernels  36.9 us (93%)
  other arithmetic  0.92 us (2%)
  between operations  0.68 us (2%)
  local copies, waits for them, and re-layouts  0.62 us (2%)
    pallas_call x1, Pallas kernels, body(): pl.pallas_call(functools.partial(kernel, blocks, members, scale), out_sha...  36.9 us
    mul x1, other arithmetic, body(): mixed_grad * keys  0.92 us

profile of v1, /device:TPU:1, one launch (start us, length us, event | category | flops | bytes accessed | tf_op | source)
XLA Modules:
  0.0 39.2 jit_solution(13062671858193441275)
XLA Ops:
  0.6 0.0 copy-start
  0.6 0.0 copy-start.1
  0.7 0.0 copy-start.2
  0.7 0.0 copy-start.3
  0.7 36.9 %shard_map.137 = (f32[128,128]{1,0:T(8,128)S(1)}, f32[128,128]{1,0:T(8,128)S(1)}, f32[16,128]{1,0:T(8,128)S(1)}) custom-call(f32[128,128]{1,0:T(8,128)} %bitcast.11, f32[128,128]{1,0:T(8,128)} %bitcast.12, f32[128,128]{1,0:T(8,128)} %bitcast.13, f32[128,128]{1,0:T(8,128)} %bitcast.15, f32[128,128]{1,0:T(8,128)} %bitcast.14, ...), custom_call_target="tpu_custom_call" | custom-call | tf_op jit(solution)/shard_map/pallas_call | solution.py:383
  37.6 0.6 %copy.16 = f32[1,2048]{1,0:T(1,128)} copy(f32[1,2048]{1,0:T(1,128)S(1)} %bitcast.8) | data formatting | bytes 16384
  38.2 0.0 copy-done
  38.2 0.0 copy-done.1
  38.2 0.0 copy-done.2
  38.2 0.0 copy-done.3
  38.2 0.9 %fusion = (f32[1,1,16384]{2,1,0:T(1,128)}, f32[1,1,16384]{2,1,0:T(1,128)}, f32[1,1,16384]{2,1,0:T(1,128)}, f32[1,1,16384]{2,1,0:T(1,128)}) fusion(f32[1,1,16384]{2,1,0:T(1,128)S(1)} %bitcast.10, f32[1,1,16384]{2,1,0:T(1,128)S(1)} %copy-done.1, f32[1,1,16384]{2,1,0:T(1,128)S(1)} %copy-done.2, f32[1,1,16384]{2,1,0:T(1,128)S(1)} %copy-done, ...), kind=kLoop, calls=%fused_computation | loop fusion | flops 65536 | bytes 655360 | tf_op jit(solution)/shard_map/mul | solution.py:406
Async XLA Ops:
  0.6 37.6 %copy-start = (f32[1,1,16384]{2,1,0:T(1,128)S(1)}, f32[1,1,16384]{2,1,0:T(1,128)}, u32[]{:S(2)}) copy-start(f32[1,1,16384]{2,1,0:T(1,128)} %param.10) | copy-start | bytes 196612
  0.6 37.6 %copy-start.1 = (f32[1,1,16384]{2,1,0:T(1,128)S(1)}, f32[1,1,16384]{2,1,0:T(1,128)}, u32[]{:S(2)}) copy-start(f32[1,1,16384]{2,1,0:T(1,128)} %param.11) | copy-start | bytes 196612
  0.7 37.6 %copy-start.2 = (f32[1,1,16384]{2,1,0:T(1,128)S(1)}, f32[1,1,16384]{2,1,0:T(1,128)}, u32[]{:S(2)}) copy-start(f32[1,1,16384]{2,1,0:T(1,128)} %param.12) | copy-start | bytes 196612
  0.7 37.6 %copy-start.3 = (f32[1,1,16384]{2,1,0:T(1,128)S(1)}, f32[1,1,16384]{2,1,0:T(1,128)}, u32[]{:S(2)}) copy-start(f32[1,1,16384]{2,1,0:T(1,128)} %param.14) | copy-start | bytes 196612

commit v2 on v1

--- a/solution.py
+++ b/solution.py
@@ -77,11 +77,10 @@
     convolved_ref, mixed_grad_ref, filter_grad_ref,
     query_ref, key_ref, value_ref, filter_ref, cotangent_ref,
     fwd_ref, inv_ref, cos_ref, sin_ref, inner_ref,
-    spectra, arrived, filter_spectra, filter_arrived,
-    results, returned, terms, terms_arrived, term_sums, term_rows, pieces, piece,
+    spectra, arrived, filter_spectra, filter_arrived, results, returned, shares,
     grads, filters, mixed, factor,
-    load_sems, pair_send, pair_recv, filter_send, filter_recv, pass_send, pass_recv,
-    terms_send, terms_recv, sums_send, sums_recv, result_send, result_recv, piece_send, piece_recv,
+    load_sems, filter_send, filter_recv, pass_send, pass_recv,
+    block_send, block_recv, share_send, share_recv,
 ):
     me = lax.axis_index("ctx")
     member = lax.axis_index("ch")
@@ -90,11 +89,17 @@
     at_y = lax.div(me, depth)
     at_z = lax.rem(me, depth)
 
+    def hops(step):
+        over_y, over_z = step // depth, step % depth
+        return min(over_y, height - over_y) + min(over_z, depth - over_z)
+
+    peers = [
+        (step, lax.rem(at_y + step // depth, height) * depth + lax.rem(at_z + step % depth, depth))
+        for step in sorted(range(1, blocks), key=lambda step: -hops(step))
+    ]
     barrier = pltpu.get_barrier_semaphore()
-    for step in range(1, blocks):
-        pl.semaphore_signal(
-            barrier, inc=1, device_id={"ctx": lax.rem(me + step, blocks)}, device_id_type=MESH
-        )
+    for _, peer in peers:
+        pl.semaphore_signal(barrier, inc=1, device_id={"ctx": peer}, device_id_type=MESH)
     for step in range(1, members):
         pl.semaphore_signal(
             barrier, inc=1, device_id={"ch": lax.rem(member + step, members)}, device_id_type=MESH
@@ -103,9 +108,9 @@
     loads = [
         pltpu.make_async_copy(source, target, load_sems.at[at])
         for at, (source, target) in enumerate((
-            (key_hbm, key_ref), (value_hbm, value_ref), (cotangent_hbm, cotangent_ref),
-            (query_hbm, query_ref), (fwd_hbm, fwd_ref), (filter_hbm, filter_ref),
-            (cos_hbm, cos_ref), (sin_hbm, sin_ref), (inner_hbm, inner_ref), (inv_hbm, inv_ref),
+            (cotangent_hbm, cotangent_ref), (query_hbm, query_ref), (filter_hbm, filter_ref),
+            (fwd_hbm, fwd_ref), (cos_hbm, cos_ref), (sin_hbm, sin_ref), (inner_hbm, inner_ref),
+            (key_hbm, key_ref), (value_hbm, value_ref), (inv_hbm, inv_ref),
         ))
     ]
     for load in loads:
@@ -139,14 +144,27 @@
             device_id=device, device_id_type=MESH,
         )
 
+    def exchange(outgoing, incoming, part):
+        copies = [
+            send(
+                outgoing.at[peer], incoming.at[me],
+                block_send.at[part, step], block_recv.at[part, step], ctx=peer,
+            )
+            for step, peer in peers
+        ]
+        for copy in copies:
+            copy.start()
+        incoming[me] = outgoing[me]
+        return copies
+
     for load in loads[:9]:
         load.wait()
-    mixed_input = key_ref[...] * value_ref[...]
-    grad_in = cotangent_ref[...] * query_ref[...]
-    filter_spectra[...] = forward([filter_ref[...]])[0]
-    pair = forward([mixed_input, grad_in])
+    pair = forward(
+        [cotangent_ref[...] * query_ref[...], key_ref[...] * value_ref[...], filter_ref[...]]
+    )
     spectra[:, 0] = pair[0]
     spectra[:, 1] = pair[1]
+    filter_spectra[...] = pair[2]
 
     pl.semaphore_wait(barrier, blocks + members - 2)
 
@@ -171,18 +189,7 @@
     def _():
         direct[0].start()
 
-    pairs = []
-    for step in range(1, blocks):
-        peer = lax.rem(me + step, blocks)
-        pairs.append(
-            send(
-                spectra.at[peer], arrived.at[me],
-                pair_send.at[step], pair_recv.at[step], ctx=peer,
-            )
-        )
-    for copy in pairs:
-        copy.start()
-    arrived[me] = spectra[me]
+    sent = exchange(spectra, arrived, 0)
 
     @pl.when(member != 0)
     def _():
@@ -236,30 +243,20 @@
             return total
         return lax.fori_loop(0, (first + depth) // unroll, add, zeros)
 
-    for copy in pairs:
-        copy.wait_recv()
-    grad = arrived[:, 1]
+    for copy in sent:
+        copy.wait_recv()
+    grad = arrived[:, 0]
     grads[0, :blocks] = grad
     grads[1, :blocks] = swap(grad)
-    mix = arrived[:, 0]
+    mix = arrived[:, 1]
     mixed[0, depth:] = mix
     mixed[1, depth:] = swap(mix)
     real, imag = factors(shifted(mix))
     factor[0] = real
     factor[1] = imag
     for row in range(height):
-        terms[:, row] = correlate(factor, row * depth)
-    reduced = []
-    for step in range(1, members):
-        peer = lax.rem(member + step, members)
-        reduced.append(
-            send(
-                terms.at[peer], terms_arrived.at[step],
-                terms_send.at[step], terms_recv.at[step], ch=peer,
-            )
-        )
-    for copy in reduced:
-        copy.start()
+        results[0, pl.ds(row * depth, depth)] = correlate(factor, row * depth)
+    sent_terms = exchange(results.at[0], returned.at[0], 1)
 
     for copy in passed:
         copy.wait_recv()
@@ -267,103 +264,51 @@
     real, imag = factors(shifted(whole))
     filters[0] = real
     filters[1] = imag
-
-    def give_back(part):
-        copies = []
-        for step in range(1, blocks):
-            peer = lax.rem(me + step, blocks)
-            copies.append(
-                send(
-                    results.at[part, peer], returned.at[part, me],
-                    result_send.at[part, step], result_recv.at[part, step], ctx=peer,
-                )
-            )
-        for copy in copies:
-            copy.start()
-        returned[part, me] = results[part, me]
-        return copies
-
     for row in range(height):
-        results[0, pl.ds(row * depth, depth)] = convolve(row * depth)
-    sent_convolved = give_back(0)
-
-    worker = at_z == member
-    for copy in reduced:
-        copy.wait_recv()
-    total = terms[member]
-    for step in range(1, members):
-        total = total + terms_arrived[step]
-    term_sums[...] = total
-    summed = []
-    for step in range(height):
-        row = lax.rem(at_y + step, height)
-        summed.append(
-            send(
-                term_sums.at[row], term_rows.at[me],
-                sums_send.at[step], sums_recv.at[me], ctx=row * depth + member,
-            )
-        )
-    for copy in summed[1:]:
-        copy.start()
-
-    @pl.when(worker)
-    def _():
-        term_rows[me] = term_sums[at_y]
-
-    @pl.when(jnp.logical_not(worker))
-    def _():
-        summed[0].start()
-
+        results[1, pl.ds(row * depth, depth)] = convolve(row * depth)
+    sent_convolved = exchange(results.at[1], returned.at[1], 2)
     for row in range(height):
-        results[1, pl.ds(row * depth, depth)] = correlate(filters, row * depth)
-    sent_grads = give_back(1)
+        results[2, pl.ds(row * depth, depth)] = correlate(filters, row * depth)
+    sent_back = exchange(results.at[2], returned.at[2], 3)
 
     loads[9].wait()
-    for copy in sent_convolved:
-        copy.wait_recv()
-    convolved_ref[...] = inverse(returned[0].reshape(-1, LANES))
-
+    for copy in sent_terms:
+        copy.wait_recv()
+    term = inverse(returned[0].reshape(-1, LANES)) * scale
+    shares[0] = term.reshape((members,) + shares.shape[2:])
     scattered = []
     for step in range(1, members):
         peer = lax.rem(member + step, members)
         scattered.append(
-            send(pieces.at[peer], piece, piece_send.at[step], piece_recv.at[0], ch=peer)
-        )
-
-    @pl.when(worker)
-    def _():
-        for step in range(1, blocks):
-            peer = lax.rem(me + step, blocks)
             send(
-                term_sums.at[0], term_rows.at[peer], sums_send.at[0], sums_recv.at[peer], ctx=peer
-            ).wait_recv()
-        term = inverse(term_rows[...].reshape(-1, LANES)) * scale
-        pieces[...] = term.reshape(pieces.shape)
-        for copy in scattered:
-            copy.start()
-        piece[...] = pieces[member]
-
-    for copy in sent_grads:
-        copy.wait_recv()
-    mixed_grad_ref[...] = inverse(returned[1].reshape(-1, LANES))
-
-    @pl.when(jnp.logical_not(worker))
-    def _():
-        scattered[0].wait_recv()
-        summed[0].wait_send()
-
-    filter_grad_ref[...] = piece[...]
-
-    @pl.when(worker)
-    def _():
-        for copy in scattered:
-            copy.wait_send()
+                shares.at[0, peer], shares.at[1, step],
+                share_send.at[step], share_recv.at[step], ch=peer,
+            )
+        )
+    for copy in scattered:
+        copy.start()
+
+    for copy in sent_convolved:
+        copy.wait_recv()
+    convolved_ref[...] = inverse(returned[1].reshape(-1, LANES))
+    for copy in sent_back:
+        copy.wait_recv()
+    mixed_grad_ref[...] = inverse(returned[2].reshape(-1, LANES))
+
+    total = shares[0, member]
+    for copy in scattered:
+        copy.wait_recv()
+    for step in range(1, members):
+        total = total + shares[1, step]
+    filter_grad_ref[...] = total
 
     @pl.when(member != 0)
     def _():
         direct[0].wait_send()
 
-    for copy in direct[1:] + pairs + passed + reduced + sent_convolved + summed[1:] + sent_grads:
+    for copy in direct[1:] + sent + passed + sent_back + sent_terms:
+        copy.wait_send()
+    for copy in sent_convolved + scattered:
         copy.wait_send()
 
 
@@ -389,14 +334,11 @@
         scratch_shapes=[pltpu.VMEM(array.shape, array.dtype) for array in arrays]
         + [
             vmem(blocks, 2), vmem(blocks, 2), vmem(blocks), vmem(members, height),
-            vmem(2, blocks), vmem(2, blocks),
-            vmem(members, height), vmem(members, height), vmem(height), vmem(blocks),
-            pltpu.VMEM((members, share, LANES), jnp.float32),
-            pltpu.VMEM((share, LANES), jnp.float32),
+            vmem(3, blocks), vmem(3, blocks),
+            pltpu.VMEM((2, members, share, LANES), jnp.float32),
             vmem(2, blocks + members), vmem(2, blocks), vmem(2, blocks + members), vmem(2, blocks),
-            dma(10), dma(blocks), dma(blocks), dma(height), dma(height), dma(members), dma(members),
-            dma(members), dma(members), dma(height), dma(blocks), dma(2, blocks), dma(2, blocks),
-            dma(members), dma(1),
+            dma(10), dma(height), dma(height), dma(members), dma(members),
+            dma(4, blocks), dma(4, blocks), dma(members), dma(members),
         ],
         compiler_params=pltpu.CompilerParams(collective_id=0, has_side_effects=True),
     )(*arrays)

time: 39.7 us -> 38.6 us (0.972); the launches traced: 39.2 us -> 38.5 us
  Pallas kernels: 36.9 us -> 36.3 us
    pallas_call x1, Pallas kernels: 36.9 us -> 36.3 us  [body(): pl.pallas_call(functools.partial(kernel, blocks, members, scale), out_sha...]
where the time goes in v2:
time: 38.6 us; the launch traced here: 38.5 us
  Pallas kernels  36.3 us (94%)
  other arithmetic  0.92 us (2%)
  between operations  0.68 us (2%)
  local copies, waits for them, and re-layouts  0.62 us (2%)
    pallas_call x1, Pallas kernels, body(): pl.pallas_call(functools.partial(kernel, blocks, members, scale), out_sha...  36.3 us
    mul x1, other arithmetic, body(): mixed_grad * keys  0.92 us

profile of v2, /device:TPU:1, one launch (start us, length us, event | category | flops | bytes accessed | tf_op | source)
XLA Modules:
  0.0 38.5 jit_solution(4446347637509734399)
XLA Ops:
  0.6 0.0 copy-start
  0.6 0.0 copy-start.1
  0.7 0.0 copy-start.2
  0.7 0.0 copy-start.3
  0.7 36.3 %shard_map.137 = (f32[128,128]{1,0:T(8,128)S(1)}, f32[128,128]{1,0:T(8,128)S(1)}, f32[16,128]{1,0:T(8,128)S(1)}) custom-call(f32[128,128]{1,0:T(8,128)} %bitcast.11, f32[128,128]{1,0:T(8,128)} %bitcast.12, f32[128,128]{1,0:T(8,128)} %bitcast.13, f32[128,128]{1,0:T(8,128)} %bitcast.15, f32[128,128]{1,0:T(8,128)} %bitcast.14, ...), custom_call_target="tpu_custom_call" | custom-call | tf_op jit(solution)/shard_map/pallas_call | solution.py:328
  37.0 0.6 %copy.16 = f32[1,2048]{1,0:T(1,128)} copy(f32[1,2048]{1,0:T(1,128)S(1)} %bitcast.8) | data formatting | bytes 16384
  37.6 0.0 copy-done
  37.6 0.0 copy-done.1
  37.6 0.0 copy-done.2
  37.6 0.0 copy-done.3
  37.6 0.9 %fusion = (f32[1,1,16384]{2,1,0:T(1,128)}, f32[1,1,16384]{2,1,0:T(1,128)}, f32[1,1,16384]{2,1,0:T(1,128)}, f32[1,1,16384]{2,1,0:T(1,128)}) fusion(f32[1,1,16384]{2,1,0:T(1,128)S(1)} %bitcast.10, f32[1,1,16384]{2,1,0:T(1,128)S(1)} %copy-done.1, f32[1,1,16384]{2,1,0:T(1,128)S(1)} %copy-done.2, f32[1,1,16384]{2,1,0:T(1,128)S(1)} %copy-done, ...), kind=kLoop, calls=%fused_computation | loop fusion | flops 65536 | bytes 655360 | tf_op jit(solution)/shard_map/mul | solution.py:348
Async XLA Ops:
  0.6 36.9 %copy-start = (f32[1,1,16384]{2,1,0:T(1,128)S(1)}, f32[1,1,16384]{2,1,0:T(1,128)}, u32[]{:S(2)}) copy-start(f32[1,1,16384]{2,1,0:T(1,128)} %param.10) | copy-start | bytes 196612
  0.6 36.9 %copy-start.1 = (f32[1,1,16384]{2,1,0:T(1,128)S(1)}, f32[1,1,16384]{2,1,0:T(1,128)}, u32[]{:S(2)}) copy-start(f32[1,1,16384]{2,1,0:T(1,128)} %param.11) | copy-start | bytes 196612
  0.7 36.9 %copy-start.2 = (f32[1,1,16384]{2,1,0:T(1,128)S(1)}, f32[1,1,16384]{2,1,0:T(1,128)}, u32[]{:S(2)}) copy-start(f32[1,1,16384]{2,1,0:T(1,128)} %param.12) | copy-start | bytes 196612
  0.7 36.9 %copy-start.3 = (f32[1,1,16384]{2,1,0:T(1,128)S(1)}, f32[1,1,16384]{2,1,0:T(1,128)}, u32[]{:S(2)}) copy-start(f32[1,1,16384]{2,1,0:T(1,128)} %param.14) | copy-start | bytes 196612
